TPU v7x, 32 devices: a whole 2x2x4 slice. The times are simulated.
32 devices in a mesh: grp: 4 (over z), dev: 8 (over y, x, core).
Axes of the slice: x: 2, y: 2, z: 4, core: 2. Of those that a mesh axis runs over, the one named last changes fastest.
Arguments:
- sources: bfloat16 [8, 131072], P(None, ('grp', 'dev')), may hold values from -6 to 6
- boundary_impedance_input: float32 [8, 256], replicated, may hold values from -6 to 6
- leaf_inverse: bfloat16 [131072, 2048], P(('grp', 'dev')), may hold values from -0.1875 to 0.1875
- leaf_flux: bfloat16 [131072, 256], P(('grp', 'dev')), may hold values from -0.1875 to 0.1875
- leaf_lift: bfloat16 [16384, 2048], P(('grp', 'dev')), may hold values from -0.375 to 0.375
- node_schur: float32 [128, 64, 128], P(('grp', 'dev')), may hold values from -0.375 to 0.375
- node_spread: float32 [128, 64, 256], P(('grp', 'dev')), may hold values from -0.1875 to 0.1875
- node_lift: float32 [128, 128, 128], P(('grp', 'dev')), may hold values from -0.25 to 0.25
Outputs:
- field: float32 [8, 262144], P(None, ('grp', 'dev'))
All inputs are finite; a program needn't handle non-finite values.
Results may differ from a plain program's by a relative error of at most 0.0025.
Values sent between devices are 32-bit elements; how exact they have to be, the bound alone decides.
A program may use at most 128 MiB of HBM per device.

v0:
```python
import jax
import jax.numpy as jnp
from jax import lax
from jax.sharding import PartitionSpec as P


def complex_mul(vector, matrix):
    inner = matrix.shape[1]
    cols = matrix.shape[2] // 2
    hp = lax.Precision.HIGHEST
    from_real = jnp.einsum("nsa,nab->nsb", vector[..., :inner], matrix, precision=hp)
    from_imag = jnp.einsum("nsa,nab->nsb", vector[..., inner:], matrix, precision=hp)
    return jnp.concatenate(
        [
            from_real[..., :cols] - from_imag[..., cols:],
            from_real[..., cols:] + from_imag[..., :cols],
        ],
        -1,
    )


def select_component(vector, start, stop):
    half = vector.shape[-1] // 2
    return jnp.concatenate([vector[..., start:stop], vector[..., half + start : half + stop]], -1)


def join_parts(first, second):
    half_one = first.shape[-1] // 2
    half_two = second.shape[-1] // 2
    return jnp.concatenate(
        [
            first[..., :half_one],
            second[..., :half_two],
            first[..., half_one:],
            second[..., half_two:],
        ],
        -1,
    )


def merge_pair(left_out, right_out, schur, spread):
    width = left_out.shape[-1] // 4
    jump = complex_mul(
        select_component(right_out, width, 2 * width)
        - select_component(left_out, width, 2 * width),
        schur,
    )
    parent = join_parts(
        select_component(left_out, 0, width), select_component(right_out, 0, width)
    ) + complex_mul(jump, spread)
    return (jump, parent)


def split_children(incoming, iface):
    width = incoming.shape[-1] // 4
    return (
        join_parts(select_component(incoming, 0, width), iface),
        join_parts(select_component(incoming, width, 2 * width), iface),
    )


def ascend(outgoing, schur, spread):
    levels = outgoing.shape[0].bit_length() - 1
    jumps = []
    for tier_index in range(levels):
        half_step = 2**tier_index
        jump, outgoing = merge_pair(
            outgoing[0::2],
            outgoing[1::2],
            schur[half_step :: 2 * half_step],
            spread[half_step :: 2 * half_step],
        )
        jumps.append(jump)
    return (outgoing, jumps)


def descend(incoming, jumps, lift):
    for tier_index in reversed(range(len(jumps))):
        half_step = 2**tier_index
        iface = complex_mul(incoming, lift[half_step :: 2 * half_step]) + jumps[tier_index]
        left_in, right_in = split_children(incoming, iface)
        incoming = jnp.stack([left_in, right_in], 1).reshape(
            -1, incoming.shape[1], incoming.shape[2]
        )
    return incoming


def body(
    sources,
    boundary_impedance_input,
    leaf_inverse,
    leaf_flux,
    leaf_lift,
    node_schur,
    node_spread,
    node_lift,
):
    source_count = sources.shape[0]
    leaves_here = node_schur.shape[0]
    cell_count = leaf_inverse.shape[1] // 2
    interface_edge_count = leaf_flux.shape[1] // 2
    source_blocks = sources.reshape(source_count, leaves_here, cell_count)
    leaf_out = jnp.einsum(
        "slc,lce->lse",
        source_blocks,
        leaf_flux.reshape(leaves_here, cell_count, 2 * interface_edge_count),
        preferred_element_type=jnp.float32,
    )
    local_root, local_jumps = ascend(leaf_out, node_schur, node_spread)
    place = lax.axis_index("grp") * lax.axis_size("dev") + lax.axis_index("dev")
    roots = lax.all_gather(local_root, ("grp", "dev"), axis=0, tiled=True)
    schur_all, spread_all, lift_all = (
        lax.all_gather(node_schur[0:1], ("grp", "dev"), axis=0, tiled=True),
        lax.all_gather(node_spread[0:1], ("grp", "dev"), axis=0, tiled=True),
        lax.all_gather(node_lift[0:1], ("grp", "dev"), axis=0, tiled=True),
    )
    top_out, tree_jumps = ascend(roots, schur_all, spread_all)
    incoming_all = descend(boundary_impedance_input[None], tree_jumps, lift_all)
    device_in = lax.dynamic_slice_in_dim(incoming_all, place, 1, 0)
    incoming = descend(device_in, local_jumps, node_lift)
    leaf_input_values = incoming.astype(jnp.bfloat16)
    particular = jnp.einsum(
        "vfz,fzo->vfo",
        source_blocks,
        leaf_inverse.reshape(leaves_here, cell_count, 2 * cell_count),
        preferred_element_type=jnp.float32,
    )
    lifting_operator = leaf_lift.reshape(leaves_here, interface_edge_count, 2 * cell_count)
    from_real = jnp.einsum(
        "kpi,kih->pkh",
        leaf_input_values[..., :interface_edge_count],
        lifting_operator,
        preferred_element_type=jnp.float32,
    )
    from_imag = jnp.einsum(
        "kpi,kih->pkh",
        leaf_input_values[..., interface_edge_count:],
        lifting_operator,
        preferred_element_type=jnp.float32,
    )
    lifted = jnp.concatenate(
        [
            from_real[..., :cell_count] - from_imag[..., cell_count:],
            from_real[..., cell_count:] + from_imag[..., :cell_count],
        ],
        -1,
    )
    field = particular + lifted
    return field.reshape(source_count, leaves_here * 2 * cell_count)


def solution(mesh):
    in_specs = (
        P(None, ("grp", "dev")),
        P(),
        P(("grp", "dev"), None),
        P(("grp", "dev"), None),
        P(("grp", "dev"), None),
        P(("grp", "dev"), None, None),
        P(("grp", "dev"), None, None),
        P(("grp", "dev"), None, None),
    )
    out_specs = P(None, ("grp", "dev"))
    return jax.shard_map(body, mesh=mesh, in_specs=in_specs, out_specs=out_specs, check_vma=False)
```

profile of v0, /device:TPU:0, one launch (start us, length us, event | category | flops | bytes accessed | tf_op | source)
XLA Modules:
  0.0 212.5 jit_solution(15684005119780731152)
XLA Ops:
  6.5 1.5 slice.828
  8.1 1.5 slice.833
  9.7 1.5 slice.768
  11.2 2.0 fusion.166
  15.3 44.0 %all_gather.13 = f32[32,8,256]{2,1,0:T(8,128)S(1)} all-gather(f32[1,8,256]{2,1,0:T(8,128)S(1)} %maximum_add_fusion.8), channel_id=1, replica_groups=mesh['grp'=4,'dev'=8] {'grp','dev'}, dimensions={0}, use_global_device_ids=true | all-gather | bytes 270336 | tf_op jit(solution)/shard_map/all_gather | solution.py:111
  59.7 7.2 %all-gather.6.cloned.1.call-done = f32[32,64,128]{2,1,0:T(8,128)} async-done(((f32[1,64,128]{2,1,0:T(8,128)}), f32[32,64,128]{2,1,0:T(8,128)}) %all-gather.6.cloned.1.call-update) | async-done | bytes 1048592 | tf_op jit(solution)/shard_map/all_gather | solution.py:113
  66.9 1.6 fusion.19
  68.5 1.6 fusion.17
  70.2 54.9 %all-gather.8.cloned.1.call-done = f32[32,64,256]{2,1,0:T(8,128)} async-done(((f32[1,64,256]{2,1,0:T(8,128)}), f32[32,64,256]{2,1,0:T(8,128)}) %all-gather.8.cloned.1.call-update) | async-done | bytes 2097168 | tf_op jit(solution)/shard_map/all_gather | solution.py:114
  125.1 1.9 fusion.5
  127.0 2.0 fusion.7
  134.3 48.9 %all-gather.4.cloned.1.call-done = f32[32,128,128]{2,1,0:T(8,128)} async-done(((f32[1,128,128]{2,1,0:T(8,128)}), f32[32,128,128]{2,1,0:T(8,128)}) %all-gather.4.cloned.1.call-update) | async-done | bytes 2097168 | tf_op jit(solution)/shard_map/all_gather | solution.py:115
  183.3 1.1 convolution_bitcast_fusion.11
  184.4 1.0 convolution_bitcast_fusion.12
  185.8 1.1 fusion.43
  186.9 1.1 fusion.41
  188.5 1.3 fusion.23
  189.8 1.3 fusion.21
  191.5 0.5 fusion.11
  192.0 0.5 fusion.9
  193.0 1.0 fusion.3
  194.0 1.0 fusion.1
  197.9 0.4 copy-done.7
  198.3 7.7 %fusion = f32[8,4,2048]{2,0,1:T(8,128)} fusion(bf16[4,1024,2048]{2,1,0:T(8,128)(2,1)} %bitcast.144, bf16[8,4,1024]{2,0,1:T(8,128)(2,1)S(1)} %bitcast.159, f32[8,4,1024]{2,0,1:T(8,128)S(1)} %get-tuple-element.6, f32[8,4,1024]{2,0,1:T(8,128)S(1)} %get-tuple-element.5), kind=kOutput, calls=%fused_computation.3 | convolution fusion | flops 134348800 | bytes 17367040 | tf_op jit(solution)/shard_map/vfz,fzo->vfo/dot_general | solution.py:122
  (142 shorter events, 12.4 us)
Async XLA Ops:
  6.5 190.6 %copy-start = (bf16[512,2048]{1,0:T(8,128)(2,1)S(1)}, bf16[512,2048]{1,0:T(8,128)(2,1)}, u32[]{:S(2)}) copy-start(bf16[512,2048]{1,0:T(8,128)(2,1)} %param.12) | copy-start | bytes 6291460
  6.5 6.8 %copy-start.6 = (f32[4,64,128]{2,1,0:T(8,128)S(1)}, f32[4,64,128]{2,1,0:T(8,128)}, u32[]{:S(2)}) copy-start(f32[4,64,128]{2,1,0:T(8,128)} %param.13) | copy-start | bytes 393220
  6.5 7.3 %copy-start.5 = (f32[4,64,256]{2,1,0:T(8,128)S(1)}, f32[4,64,256]{2,1,0:T(8,128)}, u32[]{:S(2)}) copy-start(f32[4,64,256]{2,1,0:T(8,128)} %param.14) | copy-start | bytes 786436
  6.5 60.3 %all-gather.6.cloned.1.call-start = ((), (), s32[]{:S(2)}) async-start(), calls=%async_computation.1 | async-start | bytes 1081344 | tf_op jit(solution)/shard_map/all_gather | solution.py:113
  8.1 117.0 %all-gather.8.cloned.1.call-start = ((), (), s32[]{:S(2)}) async-start(), calls=%async_computation.2 | async-start | bytes 2162688 | tf_op jit(solution)/shard_map/all_gather | solution.py:114
  9.6 173.6 %all-gather.4.cloned.1.call-start = ((), (), s32[]{:S(2)}) async-start(), calls=%async_computation | async-start | bytes 2162688 | tf_op jit(solution)/shard_map/all_gather | solution.py:115
  13.2 46.3 %copy-start.8 = (f32[8,256]{1,0:T(8,128)S(1)}, f32[8,256]{1,0:T(8,128)}, u32[]{:S(2)}) copy-start(f32[8,256]{1,0:T(8,128)} %param.9) | copy-start | bytes 24580
  125.1 4.4 %copy-start.3 = (f32[32,64,128]{2,1,0:T(8,128)S(1)}, f32[32,64,128]{2,1,0:T(8,128)}, u32[]{:S(2)}) copy-start(f32[32,64,128]{2,1,0:T(8,128)} %all-gather.6.cloned.1.call-done) | copy-start | bytes 3145732
  127.0 3.2 %copy-start.2 = (f32[32,64,256]{2,1,0:T(8,128)S(1)}, f32[32,64,256]{2,1,0:T(8,128)}, u32[]{:S(2)}) copy-start(f32[32,64,256]{2,1,0:T(8,128)} %all-gather.8.cloned.1.call-done) | copy-start | bytes 6291460
  183.3 8.2 %copy-start.1 = (f32[32,128,128]{2,1,0:T(8,128)S(1)}, f32[32,128,128]{2,1,0:T(8,128)}, u32[]{:S(2)}) copy-start(f32[32,128,128]{2,1,0:T(8,128)} %all-gather.4.cloned.1.call-done) | copy-start | bytes 6291460
  194.0 1.5 copy-start.4
  197.5 0.8 copy-start.7
Sparse Core Ops, SparseCore 0:
  10.2 56.6 all-gather.5
  69.7 55.3 all-gather.7
  128.0 55.2 all-gather.3
where the time goes:
time: 213 us
  waiting for transfers between devices  111 us (52%)
  blocking collectives  44 us (21%)
  matrix products  33.3 us (16%)
  between operations  13.4 us (6%)
  local copies, waits for them, and re-layouts  6.94 us (3%)
  other arithmetic  3.7 us (2%)
    all_gather x1, waiting for transfers between devices, body(): lax.all_gather(node_spread[0:1], ('grp', 'dev'), axis=0, tiled=True)  54.9 us
    all_gather x1, waiting for transfers between devices, body(): lax.all_gather(node_lift[0:1], ('grp', 'dev'), axis=0, tiled=True)  48.9 us
    all_gather x1, blocking collectives, body(): roots = lax.all_gather(local_root, ('grp', 'dev'), axis=0, tiled=True)  44 us
    dot_general x20, matrix products, complex_mul(): jnp.einsum('nsa,nab->nsb', vector[..., inner:], matrix, precision=hp)  11.7 us
    dot_general x20, matrix products, complex_mul(): jnp.einsum('nsa,nab->nsb', vector[..., :inner], matrix, precision=hp)  11.1 us
    dot_general x1, matrix products, body(): jnp.einsum('vfz,fzo->vfo', source_blocks, leaf_inverse.reshape(leaves_her...  7.68 us
    all_gather x1, waiting for transfers between devices, body(): lax.all_gather(node_schur[0:1], ('grp', 'dev'), axis=0, tiled=True)  7.18 us
  transfers between devices with their start and end apart: 3, of which 3 were waited for; matrix products, arithmetic and copies ran while one was open for 9% of the time, Pallas kernels for 0%

commit v1 on v0

--- a/solution.py
+++ b/solution.py
@@ -2,6 +2,18 @@
 import jax.numpy as jnp
 from jax import lax
 from jax.sharding import PartitionSpec as P
+
+
+def collect(array, axis, dim):
+    ways, here = (lax.axis_size(axis), lax.axis_index(axis))
+    grown, reach = (array, 1)
+    while reach < ways:
+        theirs = lax.ppermute(grown, axis, [(d, d ^ reach) for d in range(ways)])
+        mine_first = jnp.concatenate([grown, theirs], axis=dim)
+        theirs_first = jnp.concatenate([theirs, grown], axis=dim)
+        grown = jnp.where(here & reach == 0, mine_first, theirs_first)
+        reach = 2 * reach
+    return grown
 
 
 def complex_mul(vector, matrix):
@@ -110,7 +122,7 @@
     place = lax.axis_index("grp") * lax.axis_size("dev") + lax.axis_index("dev")
     roots = lax.all_gather(local_root, ("grp", "dev"), axis=0, tiled=True)
     schur_all, spread_all, lift_all = (
-        lax.all_gather(node_schur[0:1], ("grp", "dev"), axis=0, tiled=True),
+        collect(node_schur[0:1], ("grp", "dev"), 0),
         lax.all_gather(node_spread[0:1], ("grp", "dev"), axis=0, tiled=True),
         lax.all_gather(node_lift[0:1], ("grp", "dev"), axis=0, tiled=True),
     )

time: 213 us -> 164 us (0.77)
  waiting for transfers between devices: 111 us -> 60.7 us
  starting transfers between devices: 0.09 us -> 5.03 us
  blocking collectives: 44 us -> 41.7 us
  matrix products: 33.3 us -> 31.1 us
    all_gather x1, waiting for transfers between devices: 54.9 us -> 0.02 us  [body(): lax.all_gather(node_spread[0:1], ('grp', 'dev'), axis=0, tiled=True)]
    ppermute x0 -> x5, waiting for transfers between devices: none -> 37.5 us  [collect(): theirs = lax.ppermute(grown, axis, [(d, d ^ reach) for d in range(ways)])]
    all_gather x1, waiting for transfers between devices: 48.9 us -> 23.1 us  [body(): lax.all_gather(node_lift[0:1], ('grp', 'dev'), axis=0, tiled=True)]
    all_gather x1 -> x0, waiting for transfers between devices: 7.18 us -> none  [body(): lax.all_gather(node_schur[0:1], ('grp', 'dev'), axis=0, tiled=True)]
    ppermute x0 -> x5, starting transfers between devices: none -> 4.98 us  [collect(): theirs = lax.ppermute(grown, axis, [(d, d ^ reach) for d in range(ways)])]
    all_gather x1, blocking collectives: 44 us -> 41.7 us  [body(): roots = lax.all_gather(local_root, ('grp', 'dev'), axis=0, tiled=True)]
  transfers between devices with their start and end apart: 3 -> 7, of which waited for: 3 -> 4; matrix products, arithmetic and copies ran while one was open for 9% -> 11% of each run, Pallas kernels for 0% -> 0%
where the time goes in v1:
time: 164 us
  waiting for transfers between devices  60.7 us (37%)
  blocking collectives  41.7 us (25%)
  matrix products  31.1 us (19%)
  between operations  13.9 us (8%)
  local copies, waits for them, and re-layouts  7.23 us (4%)
  starting transfers between devices  5.03 us (3%)
  other arithmetic  3.9 us (2%)
    all_gather x1, blocking collectives, body(): roots = lax.all_gather(local_root, ('grp', 'dev'), axis=0, tiled=True)  41.7 us
    ppermute x5, waiting for transfers between devices, collect(): theirs = lax.ppermute(grown, axis, [(d, d ^ reach) for d in range(ways)])  37.5 us
    all_gather x1, waiting for transfers between devices, body(): lax.all_gather(node_lift[0:1], ('grp', 'dev'), axis=0, tiled=True)  23.1 us
    dot_general x20, matrix products, complex_mul(): jnp.einsum('nsa,nab->nsb', vector[..., inner:], matrix, precision=hp)  10.6 us
    dot_general x20, matrix products, complex_mul(): jnp.einsum('nsa,nab->nsb', vector[..., :inner], matrix, precision=hp)  10.1 us
    dot_general x1, matrix products, body(): jnp.einsum('vfz,fzo->vfo', source_blocks, leaf_inverse.reshape(leaves_her...  7.68 us
    ppermute x5, starting transfers between devices, collect(): theirs = lax.ppermute(grown, axis, [(d, d ^ reach) for d in range(ways)])  4.98 us
  transfers between devices with their start and end apart: 7, of which 4 were waited for; matrix products, arithmetic and copies ran while one was open for 11% of the time, Pallas kernels for 0%

profile of v1, /device:TPU:0, one launch (start us, length us, event | category | flops | bytes accessed | tf_op | source)
XLA Modules:
  0.0 163.5 jit_solution(10985557754695274797)
XLA Ops:
  6.5 1.6 %slice.833 = f32[1,64,256]{2,1,0:T(8,128)} slice(f32[4,64,256]{2,1,0:T(8,128)} %param.14), slice={[0:1], [0:64], [0:256]} | slice | bytes 131072 | tf_op jit(solution)/shard_map/slice | solution.py:126
  8.3 0.8 slice.828
  9.5 1.5 slice.768
  11.0 2.0 %fusion.166 = f32[4,8,256]{2,1,0:T(8,128)S(1)} fusion(bf16[8,4,1024]{2,0,1:T(8,128)(2,1)} %bitcast.158, bf16[4,1024,256]{2,1,0:T(8,128)(2,1)} %bitcast.148), kind=kOutput, calls=%fused_computation.293 | convolution fusion | flops 16777216 | bytes 2195456 | tf_op jit(solution)/shard_map/slc,lce->lse/dot_general | solution.py:115
  15.2 2.6 %collective-permute-start.1 = (f32[2,64,128]{2,1,0:T(8,128)S(1)}, f32[2,64,128]{2,1,0:T(8,128)S(1)}, u32[]{:S(2)}, u32[]{:S(2)}) collective-permute-start(f32[2,64,128]{2,1,0:T(8,128)S(1)} %maximum_select_fusion.4), channel_id=1, source_target_pairs={{0,2},{1,3},{2,0},{3,1},{4,6},{5,7},{6,4},{7,5},{8,10},{9,11},{10,... | collective-permute-start | bytes 196616 | tf_op jit(solution)/shard_map/ppermute | solution.py:11
  17.8 2.8 %collective-permute-done.1 = f32[2,64,128]{2,1,0:T(8,128)S(1)} collective-permute-done((f32[2,64,128]{2,1,0:T(8,128)S(1)}, f32[2,64,128]{2,1,0:T(8,128)S(1)}, u32[]{:S(2)}, u32[]{:S(2)}) %collective-permute-start.1) | collective-permute-done | bytes 65568 | tf_op jit(solution)/shard_map/ppermute | solution.py:11
  20.6 1.8 %collective-permute-start.2 = (f32[4,64,128]{2,1,0:T(8,128)S(1)}, f32[4,64,128]{2,1,0:T(8,128)S(1)}, u32[]{:S(2)}, u32[]{:S(2)}) collective-permute-start(f32[4,64,128]{2,1,0:T(8,128)S(1)} %maximum_select_fusion.3), channel_id=1, source_target_pairs={{0,4},{1,5},{2,6},{3,7},{4,0},{5,1},{6,2},{7,3},{8,12},{9,13},{10,... | collective-permute-start | bytes 393224 | tf_op jit(solution)/shard_map/ppermute | solution.py:11
  22.5 41.7 %all_gather.10 = f32[32,8,256]{2,1,0:T(8,128)S(1)} all-gather(f32[1,8,256]{2,1,0:T(8,128)S(1)} %maximum_add_fusion.8), channel_id=1, replica_groups=mesh['grp'=4,'dev'=8] {'grp','dev'}, dimensions={0}, use_global_device_ids=true | all-gather | bytes 270336 | tf_op jit(solution)/shard_map/all_gather | solution.py:123
  64.4 8.7 %collective-permute-done.3 = f32[8,64,128]{2,1,0:T(8,128)S(1)} collective-permute-done((f32[8,64,128]{2,1,0:T(8,128)S(1)}, f32[8,64,128]{2,1,0:T(8,128)S(1)}, u32[]{:S(2)}, u32[]{:S(2)}) %collective-permute-start.3) | collective-permute-done | bytes 262176 | tf_op jit(solution)/shard_map/ppermute | solution.py:11
  73.5 0.7 fusion.162
  74.2 26.0 %collective-permute-done.4 = f32[16,64,128]{2,1,0:T(8,128)S(1)} collective-permute-done((f32[16,64,128]{2,1,0:T(8,128)S(1)}, f32[16,64,128]{2,1,0:T(8,128)S(1)}, u32[]{:S(2)}, u32[]{:S(2)}) %collective-permute-start.4) | collective-permute-done | bytes 524320 | tf_op jit(solution)/shard_map/ppermute | solution.py:11
  100.8 0.6 fusion.17
  101.6 1.9 %fusion.5 = f32[16,8,256]{2,1,0:T(8,128)S(1)} fusion(f32[16,8,64]{2,1,0:T(8,128)S(1)} %get-tuple-element.28, f32[32,64,256]{2,1,0:T(8,128)} %all-gather.5.cloned.1.call-done), kind=kOutput, calls=%fused_computation.19 | convolution fusion | flops 25165824 | bytes 1212416 | tf_op jit(solution)/shard_map/nsa,nab->nsb/dot_general | solution.py:24
  103.5 2.0 %fusion.7 = f32[16,8,256]{2,1,0:T(8,128)S(1)} fusion(f32[16,8,64]{2,1,0:T(8,128)S(1)} %get-tuple-element.27, f32[32,64,256]{2,1,0:T(8,128)} %all-gather.5.cloned.1.call-done), kind=kOutput, calls=%fused_computation.21 | convolution fusion | flops 25165824 | bytes 1212416 | tf_op jit(solution)/shard_map/nsa,nab->nsb/dot_general | solution.py:23
  110.8 23.1 %all-gather.3.cloned.1.call-done = f32[32,128,128]{2,1,0:T(8,128)} async-done(((f32[1,128,128]{2,1,0:T(8,128)}), f32[32,128,128]{2,1,0:T(8,128)}) %all-gather.3.cloned.1.call-update) | async-done | bytes 2097168 | tf_op jit(solution)/shard_map/all_gather | solution.py:127
  133.9 1.1 convolution_bitcast_fusion.11
  135.1 1.0 convolution_bitcast_fusion.12
  136.5 1.1 fusion.43
  137.6 1.1 fusion.41
  139.1 1.3 fusion.23
  140.4 1.3 fusion.21
  143.7 1.0 fusion.3
  144.7 1.0 fusion.1
  149.0 7.7 %fusion = f32[8,4,2048]{2,0,1:T(8,128)} fusion(bf16[4,1024,2048]{2,1,0:T(8,128)(2,1)} %bitcast.144, bf16[8,4,1024]{2,0,1:T(8,128)(2,1)S(1)} %bitcast.159, f32[8,4,1024]{2,0,1:T(8,128)S(1)} %get-tuple-element.6, f32[8,4,1024]{2,0,1:T(8,128)S(1)} %get-tuple-element.5), kind=kOutput, calls=%fused_computation.3 | convolution fusion | flops 134348800 | bytes 17367040 | tf_op jit(solution)/shard_map/vfz,fzo->vfo/dot_general | solution.py:134
  (172 shorter events, 15.4 us)
Async XLA Ops:
  6.5 141.2 %copy-start = (bf16[512,2048]{1,0:T(8,128)(2,1)S(1)}, bf16[512,2048]{1,0:T(8,128)(2,1)}, u32[]{:S(2)}) copy-start(bf16[512,2048]{1,0:T(8,128)(2,1)} %param.12) | copy-start | bytes 6291460
  6.5 7.1 %copy-start.4 = (f32[4,64,256]{2,1,0:T(8,128)S(1)}, f32[4,64,256]{2,1,0:T(8,128)}, u32[]{:S(2)}) copy-start(f32[4,64,256]{2,1,0:T(8,128)} %param.14) | copy-start | bytes 786436
  6.5 6.6 %copy-start.5 = (f32[4,64,128]{2,1,0:T(8,128)S(1)}, f32[4,64,128]{2,1,0:T(8,128)}, u32[]{:S(2)}) copy-start(f32[4,64,128]{2,1,0:T(8,128)} %param.13) | copy-start | bytes 393220
  6.5 95.0 %all-gather.5.cloned.1.call-start = ((), (), s32[]{:S(2)}) async-start(), calls=%async_computation.1 | async-start | bytes 2162688 | tf_op jit(solution)/shard_map/all_gather | solution.py:126
  8.2 125.7 %all-gather.3.cloned.1.call-start = ((), (), s32[]{:S(2)}) async-start(), calls=%async_computation | async-start | bytes 2162688 | tf_op jit(solution)/shard_map/all_gather | solution.py:127
  9.0 6.2 %collective-permute-start = (f32[1,64,128]{2,1,0:T(8,128)S(1)}, f32[1,64,128]{2,1,0:T(8,128)S(1)}, u32[]{:S(2)}, u32[]{:S(2)}) collective-permute-start(f32[1,64,128]{2,1,0:T(8,128)S(1)} %slice.828), channel_id=1, source_target_pairs={{0,1},{1,0},{2,3},{3,2},{4,5},{5,4},{6,7},{7,6},{8,9},{9,8},{10,11... | collective-permute-start | bytes 98312 | tf_op jit(solution)/shard_map/ppermute | solution.py:11
  14.9 49.2 %copy-start.10 = (f32[1,8,64]{2,1,0:T(8,128)}, f32[1,8,64]{2,1,0:T(8,128)S(1)}, u32[]{:S(2)}) copy-start(f32[1,8,64]{2,1,0:T(8,128)S(1)} %get-tuple-element.155) | copy-start | bytes 6148
  14.9 49.2 %copy-start.12 = (f32[1,8,64]{2,1,0:T(8,128)}, f32[1,8,64]{2,1,0:T(8,128)S(1)}, u32[]{:S(2)}) copy-start(f32[1,8,64]{2,1,0:T(8,128)S(1)} %get-tuple-element.156) | copy-start | bytes 6148
  15.2 58.3 %copy-start.7 = (f32[8,256]{1,0:T(8,128)S(1)}, f32[8,256]{1,0:T(8,128)}, u32[]{:S(2)}) copy-start(f32[8,256]{1,0:T(8,128)} %param.9) | copy-start | bytes 24580
  15.2 5.3 %collective-permute-start.1 = (f32[2,64,128]{2,1,0:T(8,128)S(1)}, f32[2,64,128]{2,1,0:T(8,128)S(1)}, u32[]{:S(2)}, u32[]{:S(2)}) collective-permute-start(f32[2,64,128]{2,1,0:T(8,128)S(1)} %maximum_select_fusion.4), channel_id=1, source_target_pairs={{0,2},{1,3},{2,0},{3,1},{4,6},{5,7},{6,4},{7,5},{8,10},{9,11},{10,... | collective-permute-start | bytes 196616 | tf_op jit(solution)/shard_map/ppermute | solution.py:11
  20.6 43.6 %collective-permute-start.2 = (f32[4,64,128]{2,1,0:T(8,128)S(1)}, f32[4,64,128]{2,1,0:T(8,128)S(1)}, u32[]{:S(2)}, u32[]{:S(2)}) collective-permute-start(f32[4,64,128]{2,1,0:T(8,128)S(1)} %maximum_select_fusion.3), channel_id=1, source_target_pairs={{0,4},{1,5},{2,6},{3,7},{4,0},{5,1},{6,2},{7,3},{8,12},{9,13},{10,... | collective-permute-start | bytes 393224 | tf_op jit(solution)/shard_map/ppermute | solution.py:11
  64.2 9.0 %collective-permute-start.3 = (f32[8,64,128]{2,1,0:T(8,128)S(1)}, f32[8,64,128]{2,1,0:T(8,128)S(1)}, u32[]{:S(2)}, u32[]{:S(2)}) collective-permute-start(f32[8,64,128]{2,1,0:T(8,128)S(1)} %maximum_select_fusion.2), channel_id=1, source_target_pairs={{0,8},{1,9},{2,10},{3,11},{4,12},{5,13},{6,14},{7,15},{8,0},{9,1},... | collective-permute-start | bytes 786440 | tf_op jit(solution)/shard_map/ppermute | solution.py:11
  73.2 27.0 %collective-permute-start.4 = (f32[16,64,128]{2,1,0:T(8,128)S(1)}, f32[16,64,128]{2,1,0:T(8,128)S(1)}, u32[]{:S(2)}, u32[]{:S(2)}) collective-permute-start(f32[16,64,128]{2,1,0:T(8,128)S(1)} %maximum_select_fusion.1), channel_id=1, source_target_pairs={{0,16},{1,17},{2,18},{3,19},{4,20},{5,21},{6,22},{7,23},{8,24},{9,... | collective-permute-start | bytes 1572872 | tf_op jit(solution)/shard_map/ppermute | solution.py:11
  103.5 3.2 %copy-start.2 = (f32[32,64,256]{2,1,0:T(8,128)S(1)}, f32[32,64,256]{2,1,0:T(8,128)}, u32[]{:S(2)}) copy-start(f32[32,64,256]{2,1,0:T(8,128)} %all-gather.5.cloned.1.call-done) | copy-start | bytes 6291460
  107.1 29.2 %copy-start.14 = (f32[1,8,64]{2,1,0:T(8,128)S(1)}, f32[1,8,64]{2,1,0:T(8,128)}, u32[]{:S(2)}) copy-start(f32[1,8,64]{2,1,0:T(8,128)} %get-tuple-element.149) | copy-start | bytes 6148
  107.1 29.2 %copy-start.15 = (f32[1,8,64]{2,1,0:T(8,128)S(1)}, f32[1,8,64]{2,1,0:T(8,128)}, u32[]{:S(2)}) copy-start(f32[1,8,64]{2,1,0:T(8,128)} %get-tuple-element.150) | copy-start | bytes 6148
  107.1 29.2 %copy-start.16 = (f32[1,8,64]{2,1,0:T(8,128)S(1)}, f32[1,8,64]{2,1,0:T(8,128)}, u32[]{:S(2)}) copy-start(f32[1,8,64]{2,1,0:T(8,128)} %get-tuple-element.151) | copy-start | bytes 6148
  107.1 29.2 %copy-start.17 = (f32[1,8,64]{2,1,0:T(8,128)S(1)}, f32[1,8,64]{2,1,0:T(8,128)}, u32[]{:S(2)}) copy-start(f32[1,8,64]{2,1,0:T(8,128)} %get-tuple-element.152) | copy-start | bytes 6148
  133.9 8.2 %copy-start.1 = (f32[32,128,128]{2,1,0:T(8,128)S(1)}, f32[32,128,128]{2,1,0:T(8,128)}, u32[]{:S(2)}) copy-start(f32[32,128,128]{2,1,0:T(8,128)} %all-gather.3.cloned.1.call-done) | copy-start | bytes 6291460
  144.7 1.5 copy-start.3
  144.7 1.9 %copy-start.11 = (f32[1,8,64]{2,1,0:T(8,128)S(1)}, f32[1,8,64]{2,1,0:T(8,128)}, u32[]{:S(2)}) copy-start(f32[1,8,64]{2,1,0:T(8,128)} %copy-done.10) | copy-start | bytes 6148
  144.7 1.9 %copy-start.13 = (f32[1,8,64]{2,1,0:T(8,128)S(1)}, f32[1,8,64]{2,1,0:T(8,128)}, u32[]{:S(2)}) copy-start(f32[1,8,64]{2,1,0:T(8,128)} %copy-done.12) | copy-start | bytes 6148
  144.7 2.8 %copy-start.9 = (f32[2,8,64]{2,1,0:T(8,128)S(1)}, f32[2,8,64]{2,1,0:T(8,128)}, u32[]{:S(2)}) copy-start(f32[2,8,64]{2,1,0:T(8,128)} %copy-done.8) | copy-start | bytes 12292
  148.2 0.8 copy-start.6
  (1 other events, 0.6 us)
Sparse Core Ops, SparseCore 0:
  10.2 59.9 all-gather.4
  73.0 60.8 all-gather.2
